TPU v7x, 32 devices: a whole 2x2x4 slice. The times are simulated.
32 devices in a mesh: narrow: 4 (over z), wide: 8 (over y, x, core).
Axes of the slice: x: 2, y: 2, z: 4, core: 2. Of those that a mesh axis runs over, the one named last changes fastest.
Arguments:
- layer_input: bfloat16 [32, 512, 640], P(('narrow', 'wide')), may hold values from -6 to 6
- segments: int32 [32, 512], P(('narrow', 'wide')), may hold values from 0 to 7, never falling along the last dimension, each value on 1 to 192 neighbouring positions
- targets: int32 [32, 512], P(('narrow', 'wide')), may hold values from 0 to 24
- loss_mask: int32 [32, 512], P(('narrow', 'wide')), may hold values from 0 to 1
- readout: bfloat16 [640, 25], replicated, may hold values from -0.29882812 to 0.29882812
- attend_gain: bfloat16 [640], P('wide'), may hold values from 0.5 to 1.5
- attend_shift: bfloat16 [640], P('wide'), may hold values from -1.1953125 to 1.1953125
- heads_weight: bfloat16 [640, 1920], P('wide'), may hold values from -0.25 to 0.25
- query_bias: bfloat16 [640], P('wide'), may hold values from -1.1953125 to 1.1953125
- value_bias: bfloat16 [640], P('wide'), may hold values from -1.1953125 to 1.1953125
- output_weight: bfloat16 [640, 640], P('wide'), may hold values from -1.25 to 1.25
- output_bias: bfloat16 [640], P('wide'), may hold values from -1.1953125 to 1.1953125
- forward_gain: bfloat16 [640], P('wide'), may hold values from 0.5 to 1.5
- forward_shift: bfloat16 [640], P('wide'), may hold values from -1.1953125 to 1.1953125
- up_weight: bfloat16 [640, 5120], P('wide'), may hold values from -0.25 to 0.25
- up_bias: bfloat16 [5120], P('wide'), may hold values from -1.1953125 to 1.1953125
- down_weight: bfloat16 [5120, 640], P('wide'), may hold values from -0.125 to 0.125
- down_bias: bfloat16 [640], P('wide'), may hold values from -1.1953125 to 1.1953125
Outputs:
- layer_output: bfloat16 [32, 512, 640], P(('narrow', 'wide'))
- input_grad: float32 [32, 512, 640], P(('narrow', 'wide'))
- attend_gain_grad: float32 [640], P('wide')
- attend_shift_grad: float32 [640], P('wide')
- heads_weight_grad: float32 [640, 1920], P('wide')
- query_bias_grad: float32 [640], P('wide')
- value_bias_grad: float32 [640], P('wide')
- output_weight_grad: float32 [640, 640], P('wide')
- output_bias_grad: float32 [640], P('wide')
- forward_gain_grad: float32 [640], P('wide')
- forward_shift_grad: float32 [640], P('wide')
- up_weight_grad: float32 [640, 5120], P('wide')
- up_bias_grad: float32 [5120], P('wide')
- down_weight_grad: float32 [5120, 640], P('wide')
- down_bias_grad: float32 [640], P('wide')
- loss_sum: float32 [], replicated
- token_count: int32 [], replicated
All inputs are finite; a program needn't handle non-finite values.
Results may differ from a plain program's by a relative error of at most 0.013.
Values may be sent and summed in bfloat16 or wider, within the bound.
No kernel may reach another device: no remote copies, remote signals or barrier semaphores. Data moves between devices by JAX's collectives and lax.ppermute only.
A program may use at most 192 MiB of HBM per device.

v0:
```python
import math
import jax
import jax.numpy as jnp
from jax import lax
from jax.sharding import PartitionSpec as P

HEADS = 20
HEAD_DIM = 32


def normalize(values, gain, shift):
    average = jnp.mean(values, axis=-1, keepdims=True)
    centred = values - average
    spread = jnp.mean(centred * centred, axis=-1, keepdims=True)
    return centred * lax.rsqrt(spread + 1e-05) * gain + shift


def exact_gelu(values):
    return jax.nn.gelu(values, approximate=False)


def masked_scores(query_block, keyset, segment_block, segment_row):
    scale = 1.0 / math.sqrt(HEAD_DIM)
    scores = (
        jnp.einsum("qhd,khd->hqk", query_block, keyset, preferred_element_type=jnp.float32) * scale
    )
    allowed = (segment_block[:, None] == segment_row[None, :])[None]
    return jnp.where(allowed, scores, -1e30)


def local(
    layer_input,
    segments,
    targets,
    loss_mask,
    readout,
    attend_gain,
    attend_shift,
    heads_weight,
    query_bias,
    value_bias,
    output_weight,
    output_bias,
    forward_gain,
    forward_shift,
    up_weight,
    up_bias,
    down_weight,
    down_bias,
):
    length = layer_input.shape[1]
    width = layer_input.shape[2]
    block = min(512, length)
    count_blocks = length // block
    scale = 1.0 / math.sqrt(HEAD_DIM)
    inputs = layer_input[0].astype(jnp.float32)
    segment_row = segments[0]
    attend_set = (
        lax.all_gather(attend_gain, "wide", axis=0, tiled=True),
        lax.all_gather(attend_shift, "wide", axis=0, tiled=True),
        lax.all_gather(heads_weight, "wide", axis=0, tiled=True),
        lax.all_gather(query_bias, "wide", axis=0, tiled=True),
        lax.all_gather(value_bias, "wide", axis=0, tiled=True),
        lax.all_gather(output_weight, "wide", axis=0, tiled=True),
        lax.all_gather(output_bias, "wide", axis=0, tiled=True),
    )
    first_normed, first_pull = jax.vjp(
        normalize, inputs, attend_set[0].astype(jnp.float32), attend_set[1].astype(jnp.float32)
    )
    first_low = first_normed.astype(jnp.bfloat16)
    bias_row = jnp.concatenate(
        [attend_set[3], jnp.zeros_like(attend_set[3]), attend_set[4]]
    ).astype(jnp.float32)
    joined = (
        jnp.dot(first_low, attend_set[2], preferred_element_type=jnp.float32) + bias_row
    ).astype(jnp.bfloat16)
    split_heads = joined.reshape(length, 3, HEADS, HEAD_DIM)
    keyset = split_heads[:, 1]
    valueset = split_heads[:, 2]
    query_blocks = split_heads[:, 0].reshape(count_blocks, block, HEADS, HEAD_DIM)
    segment_blocks = segment_row.reshape(count_blocks, block)

    def forward_block(pieces):
        query_block, segment_block = pieces
        scores = masked_scores(query_block, keyset, segment_block, segment_row)
        highest = jnp.max(scores, axis=-1, keepdims=True)
        shifted = jnp.exp(scores - highest)
        totals = jnp.sum(shifted, axis=-1, keepdims=True)
        probs_low = (shifted / totals).astype(jnp.bfloat16)
        output = jnp.einsum("hqk,khd->qhd", probs_low, valueset, preferred_element_type=jnp.float32)
        return (output.astype(jnp.bfloat16), (highest + jnp.log(totals))[..., 0])

    attended_blocks, lse_blocks = lax.map(forward_block, (query_blocks, segment_blocks))
    attended = attended_blocks.reshape(length, width)
    middle = (
        inputs
        + jnp.dot(attended, attend_set[5], preferred_element_type=jnp.float32)
        + attend_set[6].astype(jnp.float32)
    )
    forward_set = (
        lax.all_gather(forward_gain, "wide", axis=0, tiled=True),
        lax.all_gather(forward_shift, "wide", axis=0, tiled=True),
        lax.all_gather(up_weight, "wide", axis=0, tiled=True),
        lax.all_gather(up_bias, "wide", axis=0, tiled=True),
        lax.all_gather(down_weight, "wide", axis=0, tiled=True),
        lax.all_gather(down_bias, "wide", axis=0, tiled=True),
    )
    second_normed, second_pull = jax.vjp(
        normalize, middle, forward_set[0].astype(jnp.float32), forward_set[1].astype(jnp.float32)
    )
    second_low = second_normed.astype(jnp.bfloat16)
    upward = jnp.dot(second_low, forward_set[2], preferred_element_type=jnp.float32) + forward_set[
        3
    ].astype(jnp.float32)
    activated, gelu_pull = jax.vjp(exact_gelu, upward)
    activated_low = activated.astype(jnp.bfloat16)
    result = (
        middle
        + jnp.dot(activated_low, forward_set[4], preferred_element_type=jnp.float32)
        + forward_set[5].astype(jnp.float32)
    )
    result_low = result.astype(jnp.bfloat16)
    logits = jnp.dot(result_low, readout, preferred_element_type=jnp.float32)
    highest_logit = jnp.max(logits, axis=-1, keepdims=True)
    shifted_logits = jnp.exp(logits - highest_logit)
    logit_totals = jnp.sum(shifted_logits, axis=-1, keepdims=True)
    log_total = highest_logit[:, 0] + jnp.log(logit_totals[:, 0])
    onehot = lax.broadcasted_iota(jnp.int32, logits.shape, 1) == targets[0][:, None]
    picked = jnp.sum(jnp.where(onehot, logits, 0.0), axis=-1)
    weights_row = loss_mask[0].astype(jnp.float32)
    loss_local = jnp.sum((log_total - picked) * weights_row)
    count_local = jnp.sum(weights_row)
    wide_count = lax.axis_size("wide")
    loss_column = jnp.full((wide_count,), loss_local)
    count_column = jnp.full((wide_count,), count_local)
    grad_logits = (
        weights_row[:, None] * (shifted_logits / logit_totals - onehot.astype(jnp.float32))
    ).astype(jnp.bfloat16)
    grad_result = jnp.einsum("lv,dv->ld", grad_logits, readout, preferred_element_type=jnp.float32)
    up_matrix, down_matrix = (
        lax.all_gather(up_weight, "wide", axis=0, tiled=True),
        lax.all_gather(down_weight, "wide", axis=0, tiled=True),
    )
    grad_down = grad_result.astype(jnp.bfloat16)
    down_weight_part = jnp.einsum(
        "lf,ld->fd", activated_low, grad_down, preferred_element_type=jnp.float32
    )
    down_bias_part = jnp.sum(grad_down, axis=0, dtype=jnp.float32)
    grad_activated = jnp.einsum(
        "ld,fd->lf", grad_down, down_matrix, preferred_element_type=jnp.float32
    )
    grad_up = gelu_pull(grad_activated)[0].astype(jnp.bfloat16)
    up_weight_part = jnp.einsum(
        "ld,lf->df", second_low, grad_up, preferred_element_type=jnp.float32
    )
    up_bias_part = jnp.sum(grad_up, axis=0, dtype=jnp.float32)
    grad_second = jnp.einsum("lf,df->ld", grad_up, up_matrix, preferred_element_type=jnp.float32)
    middle_part, forward_gain_part, forward_shift_part = second_pull(grad_second)
    grad_middle = grad_result + middle_part
    forward_shards = (
        lax.psum_scatter(forward_gain_part, "wide", scatter_dimension=0, tiled=True),
        lax.psum_scatter(forward_shift_part, "wide", scatter_dimension=0, tiled=True),
        lax.psum_scatter(up_weight_part, "wide", scatter_dimension=0, tiled=True),
        lax.psum_scatter(up_bias_part, "wide", scatter_dimension=0, tiled=True),
        lax.psum_scatter(down_weight_part, "wide", scatter_dimension=0, tiled=True),
        lax.psum_scatter(down_bias_part, "wide", scatter_dimension=0, tiled=True),
        lax.psum_scatter(loss_column, "wide", scatter_dimension=0, tiled=True),
        lax.psum_scatter(count_column, "wide", scatter_dimension=0, tiled=True),
    )
    heads_matrix, output_matrix = (
        lax.all_gather(heads_weight, "wide", axis=0, tiled=True),
        lax.all_gather(output_weight, "wide", axis=0, tiled=True),
    )
    grad_branch = grad_middle.astype(jnp.bfloat16)
    output_weight_part = jnp.einsum(
        "ld,le->de", attended, grad_branch, preferred_element_type=jnp.float32
    )
    output_bias_part = jnp.sum(grad_branch, axis=0, dtype=jnp.float32)
    grad_attended = jnp.einsum(
        "le,de->ld", grad_branch, output_matrix, preferred_element_type=jnp.float32
    ).astype(jnp.bfloat16)
    grad_blocks = grad_attended.reshape(count_blocks, block, HEADS, HEAD_DIM)

    def backward_block(carry, pieces):
        key_sum, value_sum = carry
        query_block, segment_block, grad_block, lse_block = pieces
        scores = masked_scores(query_block, keyset, segment_block, segment_row)
        probs = jnp.exp(scores - lse_block[..., None])
        value_sum = value_sum + jnp.einsum(
            "hqk,qhd->khd",
            probs.astype(jnp.bfloat16),
            grad_block,
            preferred_element_type=jnp.float32,
        )
        grad_probs = jnp.einsum(
            "qhd,khd->hqk", grad_block, valueset, preferred_element_type=jnp.float32
        )
        inner = jnp.sum(probs * grad_probs, axis=-1, keepdims=True)
        grad_scores = (probs * (grad_probs - inner)).astype(jnp.bfloat16)
        grad_query = (
            jnp.einsum("hqk,khd->qhd", grad_scores, keyset, preferred_element_type=jnp.float32)
            * scale
        )
        key_sum = (
            key_sum
            + jnp.einsum(
                "hqk,qhd->khd", grad_scores, query_block, preferred_element_type=jnp.float32
            )
            * scale
        )
        return ((key_sum, value_sum), grad_query)

    zero_heads = jnp.zeros((length, HEADS, HEAD_DIM), jnp.float32)
    (key_sum, value_sum), query_grads = lax.scan(
        backward_block,
        (zero_heads, zero_heads),
        (query_blocks, segment_blocks, grad_blocks, lse_blocks),
    )
    grad_joined = jnp.concatenate(
        [
            query_grads.reshape(length, width),
            key_sum.reshape(length, width),
            value_sum.reshape(length, width),
        ],
        axis=1,
    ).astype(jnp.bfloat16)
    heads_weight_part = jnp.einsum(
        "ld,le->de", first_low, grad_joined, preferred_element_type=jnp.float32
    )
    query_bias_part = jnp.sum(grad_joined[:, :width], axis=0, dtype=jnp.float32)
    value_bias_part = jnp.sum(grad_joined[:, 2 * width :], axis=0, dtype=jnp.float32)
    grad_first = jnp.einsum(
        "le,de->ld", grad_joined, heads_matrix, preferred_element_type=jnp.float32
    )
    input_part, attend_gain_part, attend_shift_part = first_pull(grad_first)
    input_grad = grad_middle + input_part
    attend_shards = (
        lax.psum_scatter(attend_gain_part, "wide", scatter_dimension=0, tiled=True),
        lax.psum_scatter(attend_shift_part, "wide", scatter_dimension=0, tiled=True),
        lax.psum_scatter(heads_weight_part, "wide", scatter_dimension=0, tiled=True),
        lax.psum_scatter(query_bias_part, "wide", scatter_dimension=0, tiled=True),
        lax.psum_scatter(value_bias_part, "wide", scatter_dimension=0, tiled=True),
        lax.psum_scatter(output_weight_part, "wide", scatter_dimension=0, tiled=True),
        lax.psum_scatter(output_bias_part, "wide", scatter_dimension=0, tiled=True),
    )
    summed = (
        lax.psum(attend_shards[0].astype(jnp.bfloat16), "narrow").astype(jnp.float32),
        lax.psum(attend_shards[1].astype(jnp.bfloat16), "narrow").astype(jnp.float32),
        lax.psum(attend_shards[2].astype(jnp.bfloat16), "narrow").astype(jnp.float32),
        lax.psum(attend_shards[3].astype(jnp.bfloat16), "narrow").astype(jnp.float32),
        lax.psum(attend_shards[4].astype(jnp.bfloat16), "narrow").astype(jnp.float32),
        lax.psum(attend_shards[5].astype(jnp.bfloat16), "narrow").astype(jnp.float32),
        lax.psum(attend_shards[6].astype(jnp.bfloat16), "narrow").astype(jnp.float32),
        lax.psum(forward_shards[0].astype(jnp.bfloat16), "narrow").astype(jnp.float32),
        lax.psum(forward_shards[1].astype(jnp.bfloat16), "narrow").astype(jnp.float32),
        lax.psum(forward_shards[2].astype(jnp.bfloat16), "narrow").astype(jnp.float32),
        lax.psum(forward_shards[3].astype(jnp.bfloat16), "narrow").astype(jnp.float32),
        lax.psum(forward_shards[4].astype(jnp.bfloat16), "narrow").astype(jnp.float32),
        lax.psum(forward_shards[5].astype(jnp.bfloat16), "narrow").astype(jnp.float32),
        lax.psum(forward_shards[6].astype(jnp.bfloat16), "narrow").astype(jnp.float32),
        lax.psum(forward_shards[7].astype(jnp.bfloat16), "narrow").astype(jnp.float32),
    )
    loss_total = summed[13][0]
    count_total = summed[14][0]
    return (
        result_low[None],
        input_grad[None],
        summed[0],
        summed[1],
        summed[2],
        summed[3],
        summed[4],
        summed[5],
        summed[6],
        summed[7],
        summed[8],
        summed[9],
        summed[10],
        summed[11],
        summed[12],
        loss_total,
        count_total.astype(jnp.int32),
    )


def solution(mesh):
    in_specs = (
        P(("narrow", "wide"), None, None),
        P(("narrow", "wide"), None),
        P(("narrow", "wide"), None),
        P(("narrow", "wide"), None),
        P(),
        P("wide"),
        P("wide"),
        P("wide", None),
        P("wide"),
        P("wide"),
        P("wide", None),
        P("wide"),
        P("wide"),
        P("wide"),
        P("wide", None),
        P("wide"),
        P("wide", None),
        P("wide"),
    )
    out_specs = (
        P(("narrow", "wide"), None, None),
        P(("narrow", "wide"), None, None),
        P("wide"),
        P("wide"),
        P("wide", None),
        P("wide"),
        P("wide"),
        P("wide", None),
        P("wide"),
        P("wide"),
        P("wide"),
        P("wide", None),
        P("wide"),
        P("wide", None),
        P("wide"),
        P(),
        P(),
    )
    return jax.shard_map(local, mesh=mesh, in_specs=in_specs, out_specs=out_specs, check_vma=False)
```

profile of v0, /device:TPU:0, one launch (start us, length us, event | category | flops | bytes accessed | tf_op | source)
XLA Modules:
  0.0 585.1 jit_solution(7206739429165697035)
XLA Ops:
  22.8 26.0 %all-reduce.20 = (bf16[640]{0:T(1024)(128)(2,1)S(1)}, bf16[640]{0:T(1024)(128)(2,1)S(1)}, bf16[640]{0:T(1024)(128)(2,1)S(1)}, bf16[640]{0:T(1024)(128)(2,1)S(1)}...) all-reduce(bf16[640]{0:T(1024)(128)(2,1)S(1)} %dynamic-update-slice, ...), channel_id=1, replica_groups=mesh['narrow'=4,'wide'=8] {'wide'}, use_global_device_ids=true, to_apply=%add.3 | all-reduce | flops 5120 | bytes 20480
  48.9 8.2 %all-gather = bf16[8,1,640]{2,1,0:T(2,128)(2,1)S(1)} all-gather(bf16[1,1,640]{2,1,0:T(2,128)(2,1)S(1)} %reshape.230), channel_id=1, replica_groups=mesh['narrow'=4,'wide'=8] {'wide'}, dimensions={0}, use_global_device_ids=true | all-gather | bytes 11520 | tf_op jit(solution)/shard_map/all_gather | solution.py:104
  58.1 12.7 %all_gather.48 = bf16[640,640]{1,0:T(8,128)(2,1)} all-gather(bf16[80,640]{1,0:T(8,128)(2,1)} %param.28), channel_id=1, replica_groups=mesh['narrow'=4,'wide'=8] {'wide'}, dimensions={0}, use_global_device_ids=true | all-gather | bytes 921600 | tf_op jit(solution)/shard_map/all_gather | solution.py:64
  70.8 5.1 add_convert_fusion.1
  85.3 4.1 copy-done.2
  89.4 3.9 fusion.28
  94.7 31.0 %multiply_convert_fusion.1 = (bf16[512,5120]{1,0:T(8,128)(2,1)}, f32[512,5120]{1,0:T(8,128)}, f32[512,5120]{1,0:T(8,128)}) fusion(f32[5120]{0:T(1024)S(1)} %bitcast.122, bf16[640,5120]{1,0:T(8,128)(2,1)} %all-gather.7.cloned.1.call-done, f32[512,640]{1,0:T(8,128)S(1)} %get-tuple-element.124, f32[640]{0:T(1024)S(1)} %convert_element_type.218, ...), kind=kOutput, calls=%fused_computation.14 | convolution fusion | flops 3530096640 | bytes 34108416 | tf_op jit(solution)/shard_map/dot_general | solution.py:112
  125.8 13.2 %all-gather.9.cloned.1.call-done = bf16[5120,640]{1,0:T(8,128)(2,1)} async-done(((bf16[640,640]{1,0:T(8,128)(2,1)}), bf16[5120,640]{1,0:T(8,128)(2,1)}) %all-gather.9.cloned.1.call-update) | async-done | bytes 6553616 | tf_op jit(solution)/shard_map/all_gather | solution.py:105
  139.0 8.7 %fusion.24 = bf16[512,640]{1,0:T(8,128)(2,1)S(1)} fusion(f32[512,640]{1,0:T(8,128)S(1)} %get-tuple-element.124, bf16[512,5120]{1,0:T(8,128)(2,1)} %get-tuple-element.115, bf16[5120,640]{1,0:T(8,128)(2,1)} %all-gather.9.cloned.1.call-done, f32[640]{0:T(1024)S(1)} %convert_element_type.222), kind=kOutput, calls=%fused_computation.50 | convolution fusion | flops 3356426240 | bytes 13765120 | tf_op jit(solution)/shard_map/dot_general | solution.py:119
  148.5 14.6 %convert_reduce_fusion = (f32[5120]{0:T(1024)S(1)}, bf16[512,5120]{1,0:T(8,128)(2,1)}) fusion(f32[512,5120]{1,0:T(8,128)} %get-tuple-element.116, bf16[5120,640]{1,0:T(8,128)(2,1)} %all-gather.9.cloned.1.call-done, f32[512,640]{1,0:T(8,128)S(1)} %fusion.39, f32[512,5120]{1,0:T(8,128)} %get-tuple-element.125, f32[5120]{0:T(1024)S(1)} %bitcast.123), kind=kOutput, calls=%fused_computation.11 | convolution fusion | flops 3400330240 | bytes 34119680 | tf_op jit(solution)/shard_map/ld,fd->lf/dot_general | solution.py:149
  163.1 8.5 %multiply_reduce_fusion.1 = (f32[640]{0:T(1024)S(1)}, f32[512]{0:T(512)S(1)}, f32[640]{0:T(1024)S(1)}, f32[512,640]{1,0:T(8,128)S(1)}) fusion(f32[512,640]{1,0:T(8,128)S(1)} %copy-done.4, f32[512]{0:T(512)S(1)} %fusion.45, f32[512]{0:T(512)S(1)} %broadcast_multiply_fusion, f32[640]{0:T(1024)S(1)} %convert_element_type.217, ...), kind=kOutput, calls=%fused_computation.60 | convolution fusion | flops 3358063104 | bytes 14431744 | tf_op jit(solution)/shard_map/lf,df->ld/dot_general | solution.py:157
  179.3 13.9 %multiply_reduce_fusion = (f32[20,512]{1,0:T(8,128)S(1)}, f32[20,512,512]{1,2,0:T(8,128)}) fusion(f32[20,512,512]{1,2,0:T(8,128)} %copy-done.2, f32[20,512]{1,0:T(8,128)S(1)} %log_add_fusion, bf16[512,20,32]{0,2,1:T(8,128)(2,1)} %bitcast.111, bf16[512,3,20,32]{0,3,2,1:T(8,128)(2,1)S(1)} %bitcast.108), kind=kOutput, calls=%fused_computation.1 | convolution fusion | flops 351262720 | bytes 43343872 | tf_op jit(solution)/shard_map/while/body/eval_jaxpr/qhd,khd->hqk/dot_general | solution.py:195
  193.2 14.9 %multiply_convert_fusion = bf16[20,512,512]{1,2,0:T(8,128)(2,1)S(1)} fusion(f32[20,512,512]{1,2,0:T(8,128)} %get-tuple-element.130, f32[20,512,512]{1,2,0:T(8,128)} %copy-done.2, f32[20,512]{1,0:T(8,128)S(1)} %get-tuple-element.129, f32[20,512]{1,0:T(8,128)S(1)} %log_add_fusion), kind=kLoop, calls=%fused_computation | loop fusion | flops 20971520 | bytes 52510720 | tf_op jit(solution)/shard_map/while/body/eval_jaxpr/convert_element_type | solution.py:199
  212.9 9.1 %fusion.25 = bf16[20,32,512]{2,1,0:T(8,128)(2,1)S(1)} fusion(bf16[512,20,32]{0,2,1:T(8,128)(2,1)S(1)} %bitcast.112, f32[20,512,512]{1,2,0:T(8,128)} %copy-done.2, f32[20,512]{1,0:T(8,128)S(1)} %log_add_fusion), kind=kOutput, calls=%fused_computation.51 | convolution fusion | flops 346357760 | bytes 22323200 | tf_op jit(solution)/shard_map/while/body/eval_jaxpr/hqk,qhd->khd/dot_general | solution.py:189
  222.8 4.1 fusion.34
  228.3 12.3 %fusion.57 = f32[640,5120]{1,0:T(8,128)} fusion(bf16[512,5120]{1,0:T(8,128)(2,1)} %get-tuple-element.133, f32[512,640]{1,0:T(8,128)S(1)} %copy-done.5, f32[640]{0:T(1024)S(1)} %convert_element_type.218, f32[640]{0:T(1024)S(1)} %convert_element_type.217, f32[512]{0:T(512)S(1)} %fusion.45, f32[512]{0:T(512)S(1)} %broadcast_multiply_fusion), kind=kOutput, calls=%fused_computation.117 | convolution fusion | flops 3357081600 | bytes 19670016 | tf_op jit(solution)/shard_map/ld,lf->df/dot_general | solution.py:153
  240.6 12.1 %fusion.48 = f32[5120,640]{1,0:T(8,128)} fusion(bf16[512,5120]{1,0:T(8,128)(2,1)} %get-tuple-element.115, f32[512,640]{1,0:T(8,128)S(1)} %fusion.39), kind=kOutput, calls=%fused_computation.111 | convolution fusion | flops 3355770880 | bytes 19660800 | tf_op jit(solution)/shard_map/lf,ld->fd/dot_general | solution.py:145
  254.7 27.3 %reduce-scatter.5.cloned.1.call-done = f32[80,1920]{1,0:T(8,128)} async-done(((f32[640,1920]{1,0:T(8,128)}), f32[80,1920]{1,0:T(8,128)}) %reduce-scatter.5.cloned.1.call-update) | async-done | bytes 614416 | tf_op jit(solution)/shard_map/reduce_scatter | solution.py:240
  283.9 96.4 %reduce-scatter.9.cloned.1.call-done = f32[80,5120]{1,0:T(8,128)} async-done(((f32[640,5120]{1,0:T(8,128)}), f32[80,5120]{1,0:T(8,128)}) %reduce-scatter.9.cloned.1.call-update) | async-done | bytes 1638416 | tf_op jit(solution)/shard_map/reduce_scatter | solution.py:163
  382.7 95.9 %reduce-scatter.11.cloned.1.call-done = f32[640,640]{1,0:T(8,128)} async-done(((f32[5120,640]{1,0:T(8,128)}), f32[640,640]{1,0:T(8,128)}) %reduce-scatter.11.cloned.1.call-update) | async-done | bytes 1638416 | tf_op jit(solution)/shard_map/reduce_scatter | solution.py:165
  483.9 4.0 fusion.59
  491.6 25.0 %all-reduce.19 = (bf16[640]{0:T(1024)(128)(2,1)S(1)}, bf16[640]{0:T(1024)(128)(2,1)S(1)}, bf16[640]{0:T(1024)(128)(2,1)S(1)}, bf16[640]{0:T(1024)(128)(2,1)S(1)}...) all-reduce(f32[640]{0:T(1024)S(1)} %get-tuple-element.70, ...), channel_id=2, replica_groups=mesh['narrow'=4,'wide'=8] {'wide'}, use_global_device_ids=true, to_apply=%region_14.15.clone | all-reduce | flops 10256 | bytes 61536
  519.8 12.4 %all-reduce.21 = (bf16[80]{0:T(256)(128)(2,1)S(1)}, bf16[80]{0:T(256)(128)(2,1)S(1)}, bf16[80]{0:T(256)(128)(2,1)S(1)}, bf16[80]{0:T(256)(128)(2,1)S(1)}, bf16[8...) all-reduce(bf16[80]{0:T(256)(128)(2,1)S(1)} %dynamic-slice.47, ...), channel_id=1, replica_groups=mesh['narrow'=4,'wide'=8] {'narrow'}, use_global_device_ids=true, to_apply=%region_15.16 | all-reduce | flops 1282 | bytes 5128 | tf_op jit(solution)/shard_map/psum | solution.py:247
  538.2 29.3 %all-reduce.25.cloned.1.call-done = (bf16[80,1920]{1,0:T(8,128)(2,1)}, bf16[80,640]{1,0:T(8,128)(2,1)}, bf16[80,5120]{1,0:T(8,128)(2,1)}, bf16[640,640]{1,0:T(8,128)(2,1)}) async-done(((bf16[80,1920]{1,0:T(8,128)(2,1)}, bf16[80,640]{1,0:T(8,128)(2,1)}, bf16[80,5120]{1,0:T(8,128)(2,1)}, bf16[640,640]{1,0:T(8,128)(2,1)}), (bf16[80,1920]{1,0:T(8,128)(2,1)}, bf16[80,640]{1,0:T(8,128)(2,1)}, ...) | async-done | bytes 2048016 | tf_op jit(solution)/shard_map/psum | solution.py:249
  (174 shorter events, 71.8 us)
Async XLA Ops:
  7.2 140.5 %copy-start = (bf16[640,25]{0,1:T(8,128)(2,1)S(1)}, bf16[640,25]{0,1:T(8,128)(2,1)}, u32[]{:S(2)}) copy-start(bf16[640,25]{0,1:T(8,128)(2,1)} %param.22) | copy-start | bytes 96004
  7.2 63.6 %all-gather.5.cloned.1.call-start = ((), (), s32[]{:S(2)}) async-start(), calls=%async_computation.4 | async-start | bytes 2764800 | tf_op jit(solution)/shard_map/all_gather | solution.py:61
  7.9 86.8 %all-gather.7.cloned.1.call-start = ((), (), s32[]{:S(2)}) async-start(), calls=%async_computation.5 | async-start | bytes 7372800 | tf_op jit(solution)/shard_map/all_gather | solution.py:103
  8.7 130.3 %all-gather.9.cloned.1.call-start = ((), (), s32[]{:S(2)}) async-start(), calls=%async_computation.6 | async-start | bytes 7372800 | tf_op jit(solution)/shard_map/all_gather | solution.py:105
  9.4 243.6 %reduce-scatter.7.cloned.1.call-start = ((), (), s32[]{:S(2)}) async-start(), calls=%async_computation.8 | async-start | bytes 1843200 | tf_op jit(solution)/shard_map/reduce_scatter | solution.py:243
  11.4 64.5 %copy-start.23 = (f32[512]{0:T(512)}, f32[512]{0:T(512)S(1)}, u32[]{:S(2)}) copy-start(f32[512]{0:T(512)S(1)} %broadcast_multiply_fusion.1) | copy-start | bytes 6148
  13.4 62.5 %copy-start.27 = (f32[512]{0:T(512)}, f32[512]{0:T(512)S(1)}, u32[]{:S(2)}) copy-start(f32[512]{0:T(512)S(1)} %fusion.44) | copy-start | bytes 6148
  48.8 27.1 %copy-start.21 = (f32[640]{0:T(1024)}, f32[640]{0:T(1024)S(1)}, u32[]{:S(2)}) copy-start(f32[640]{0:T(1024)S(1)} %convert_element_type.208) | copy-start | bytes 7684
  48.8 27.1 %copy-start.31 = (f32[640]{0:T(1024)}, f32[640]{0:T(1024)S(1)}, u32[]{:S(2)}) copy-start(f32[640]{0:T(1024)S(1)} %convert_element_type.209) | copy-start | bytes 7684
  94.3 44.7 %copy-start.3 = (f32[512,640]{1,0:T(8,128)}, f32[512,640]{1,0:T(8,128)S(1)}, u32[]{:S(2)}) copy-start(f32[512,640]{1,0:T(8,128)S(1)} %get-tuple-element.124) | copy-start | bytes 3932164
  148.5 14.6 %copy-start.4 = (f32[512,640]{1,0:T(8,128)S(1)}, f32[512,640]{1,0:T(8,128)}, u32[]{:S(2)}) copy-start(f32[512,640]{1,0:T(8,128)} %copy-done.3) | copy-start | bytes 3932164
  179.3 102.8 %reduce-scatter.5.cloned.1.call-start = ((), (), s32[]{:S(2)}) async-start(), calls=%async_computation.7 | async-start | bytes 5529600 | tf_op jit(solution)/shard_map/reduce_scatter | solution.py:240
  209.6 12.4 %copy-start.11 = (bf16[20,32,512]{2,1,0:T(8,128)(2,1)}, bf16[20,32,512]{2,1,0:T(8,128)(2,1)S(1)}, u32[]{:S(2)}) copy-start(bf16[20,32,512]{2,1,0:T(8,128)(2,1)S(1)} %fusion.22) | copy-start | bytes 1966084
  212.8 10.0 %copy-start.9 = (bf16[1,512,640]{2,1,0:T(8,128)(2,1)S(1)}, bf16[1,512,640]{2,1,0:T(8,128)(2,1)}, u32[]{:S(2)}) copy-start(bf16[1,512,640]{2,1,0:T(8,128)(2,1)} %param.18) | copy-start | bytes 1966084
  212.8 10.0 %copy-start.22 = (f32[640]{0:T(1024)S(1)}, f32[640]{0:T(1024)}, u32[]{:S(2)}) copy-start(f32[640]{0:T(1024)} %copy-done.21) | copy-start | bytes 7684
  212.8 10.0 %copy-start.24 = (f32[512]{0:T(512)S(1)}, f32[512]{0:T(512)}, u32[]{:S(2)}) copy-start(f32[512]{0:T(512)} %copy-done.23) | copy-start | bytes 6148
  212.8 10.0 %copy-start.28 = (f32[512]{0:T(512)S(1)}, f32[512]{0:T(512)}, u32[]{:S(2)}) copy-start(f32[512]{0:T(512)} %copy-done.27) | copy-start | bytes 6148
  227.0 153.3 %reduce-scatter.9.cloned.1.call-start = ((), (), s32[]{:S(2)}) async-start(), calls=%async_computation.9 | async-start | bytes 14745600 | tf_op jit(solution)/shard_map/reduce_scatter | solution.py:163
  240.5 238.0 %reduce-scatter.11.cloned.1.call-start = ((), (), s32[]{:S(2)}) async-start(), calls=%async_computation.10 | async-start | bytes 14745600 | tf_op jit(solution)/shard_map/reduce_scatter | solution.py:165
  252.7 229.6 %copy-start.30 = (s32[1,512]{1,0:T(1,128)S(1)}, s32[1,512]{1,0:T(1,128)}, u32[]{:S(2)}) copy-start(s32[1,512]{1,0:T(1,128)} %param.21) | copy-start | bytes 6148
  252.7 230.8 %copy-start.12 = (bf16[20,32,512]{2,1,0:T(8,128)(2,1)S(1)}, bf16[20,32,512]{2,1,0:T(8,128)(2,1)}, u32[]{:S(2)}) copy-start(bf16[20,32,512]{2,1,0:T(8,128)(2,1)} %copy-done.11) | copy-start | bytes 1966084
  252.7 230.8 %copy-start.14 = (bf16[20,32,512]{2,1,0:T(8,128)(2,1)S(1)}, bf16[20,32,512]{2,1,0:T(8,128)(2,1)}, u32[]{:S(2)}) copy-start(bf16[20,32,512]{2,1,0:T(8,128)(2,1)} %copy-done.13) | copy-start | bytes 1966084
  252.8 314.8 %all-reduce.25.cloned.1.call-start = ((), (), s32[]{:S(2)}) async-start(), calls=%async_computation.11 | async-start | bytes 4096000 | tf_op jit(solution)/shard_map/psum | solution.py:249
  488.6 87.2 %copy-start.1 = (bf16[640,25]{0,1:T(8,128)(2,1)S(1)}, bf16[640,25]{0,1:T(8,128)(2,1)}, u32[]{:S(2)}) copy-start(bf16[640,25]{0,1:T(8,128)(2,1)} %param.22) | copy-start | bytes 96004
  (17 other events, 66.8 us)
Sparse Core Ops, SparseCore 0:
  9.9 32.1 all-gather.4
  44.0 46.4 all-gather.6
  92.4 46.5 all-gather.8
  179.4 38.6 reduce-scatter.6
  227.1 54.9 reduce-scatter.4
  285.5 94.6 reduce-scatter.8
  383.8 94.6 reduce-scatter.10
  482.4 85.1 all-reduce.24
where the time goes:
time: 589 us; the launch traced here: 585 us
  waiting for transfers between devices  264 us (45%)
  matrix products  141 us (24%)
  blocking collectives  84.4 us (14%)
  other arithmetic  48.7 us (8%)
  local copies, waits for them, and re-layouts  25.6 us (4%)
  between operations  20.5 us (3%)
    reduce_scatter x1, waiting for transfers between devices, local(): lax.psum_scatter(up_weight_part, 'wide', scatter_dimension=0, tiled=True)  96.4 us
    reduce_scatter x1, waiting for transfers between devices, local(): lax.psum_scatter(down_weight_part, 'wide', scatter_dimension=0, tiled=True)  95.9 us
    unnamed x2, blocking collectives  51 us
    dot_general x1, matrix products, local(): jnp.dot(second_low, forward_set[2], preferred_element_type=jnp.float32)  31 us
    psum x1, waiting for transfers between devices, local(): lax.psum(attend_shards[2].astype(jnp.bfloat16), 'narrow')  29.3 us
    reduce_scatter x1, waiting for transfers between devices, local(): lax.psum_scatter(heads_weight_part, 'wide', scatter_dimension=0, tiled=True)  27.3 us
    unnamed x96, local copies, waits for them, and re-layouts  19.4 us
    convert_element_type x1, other arithmetic, backward_block(): grad_scores = (probs * (grad_probs - inner)).astype(jnp.bfloat16)  14.9 us
  transfers between devices with their start and end apart: 8, of which 5 were waited for; matrix products, arithmetic and copies ran while one was open for 27% of the time, Pallas kernels for 0%

commit v1 on v0

--- a/solution.py
+++ b/solution.py
@@ -6,6 +6,18 @@
 
 HEADS = 20
 HEAD_DIM = 32
+
+
+def collect(array, axis, dim):
+    ways, here = (lax.axis_size(axis), lax.axis_index(axis))
+    grown, reach = (array, 1)
+    while reach < ways:
+        theirs = lax.ppermute(grown, axis, [(d, d ^ reach) for d in range(ways)])
+        mine_first = jnp.concatenate([grown, theirs], axis=dim)
+        theirs_first = jnp.concatenate([theirs, grown], axis=dim)
+        grown = jnp.where(here & reach == 0, mine_first, theirs_first)
+        reach = 2 * reach
+    return grown
 
 
 def normalize(values, gain, shift):
@@ -102,7 +114,7 @@
         lax.all_gather(forward_shift, "wide", axis=0, tiled=True),
         lax.all_gather(up_weight, "wide", axis=0, tiled=True),
         lax.all_gather(up_bias, "wide", axis=0, tiled=True),
-        lax.all_gather(down_weight, "wide", axis=0, tiled=True),
+        collect(down_weight, "wide", 0),
         lax.all_gather(down_bias, "wide", axis=0, tiled=True),
     )
     second_normed, second_pull = jax.vjp(

time: 589 us -> 661 us (1.12)
  blocking collectives: 84.4 us -> 122 us
  waiting for transfers between devices: 264 us -> 297 us
    ppermute x0 -> x3, waiting for transfers between devices: none -> 46.6 us  [collect(): theirs = lax.ppermute(grown, axis, [(d, d ^ reach) for d in range(ways)])]
    unnamed x2, blocking collectives: 51 us -> 87.5 us
    all_gather x1, waiting for transfers between devices: 13.2 us -> 0.02 us  [local(): lax.all_gather(down_weight, 'wide', axis=0, tiled=True)]
    select_n x0 -> x2, other arithmetic: none -> 6.66 us  [collect(): grown = jnp.where(here & reach == 0, mine_first, theirs_first)]
    unnamed x96 -> x130, local copies, waits for them, and re-layouts: 19.4 us -> 13.1 us
  transfers between devices with their start and end apart: 8 -> 11, of which waited for: 5 -> 6; matrix products, arithmetic and copies ran while one was open for 27% -> 25% of each run, Pallas kernels for 0% -> 0%
where the time goes in v1:
time: 661 us; the launch traced here: 657 us
  waiting for transfers between devices  297 us (45%)
  matrix products  141 us (21%)
  blocking collectives  122 us (18%)
  other arithmetic  51.3 us (8%)
  between operations  20.8 us (3%)
  local copies, waits for them, and re-layouts  19.3 us (3%)
    reduce_scatter x1, waiting for transfers between devices, local(): lax.psum_scatter(up_weight_part, 'wide', scatter_dimension=0, tiled=True)  96.4 us
    reduce_scatter x1, waiting for transfers between devices, local(): lax.psum_scatter(down_weight_part, 'wide', scatter_dimension=0, tiled=True)  95.9 us
    unnamed x2, blocking collectives  87.5 us
    ppermute x3, waiting for transfers between devices, collect(): theirs = lax.ppermute(grown, axis, [(d, d ^ reach) for d in range(ways)])  46.6 us
    dot_general x1, matrix products, local(): jnp.dot(second_low, forward_set[2], preferred_element_type=jnp.float32)  30.6 us
    psum x1, waiting for transfers between devices, local(): lax.psum(attend_shards[2].astype(jnp.bfloat16), 'narrow')  29.3 us
    reduce_scatter x1, waiting for transfers between devices, local(): lax.psum_scatter(heads_weight_part, 'wide', scatter_dimension=0, tiled=True)  27.5 us
    convert_element_type x1, other arithmetic, backward_block(): grad_scores = (probs * (grad_probs - inner)).astype(jnp.bfloat16)  14.9 us
  transfers between devices with their start and end apart: 11, of which 6 were waited for; matrix products, arithmetic and copies ran while one was open for 25% of the time, Pallas kernels for 0%

profile of v1, /device:TPU:0, one launch (start us, length us, event | category | flops | bytes accessed | tf_op | source)
XLA Modules:
  0.0 657.0 jit_solution(14458966337452110803)
XLA Ops:
  19.8 62.5 %all-reduce.20 = (bf16[640]{0:T(1024)(128)(2,1)S(1)}, bf16[640]{0:T(1024)(128)(2,1)S(1)}, bf16[640]{0:T(1024)(128)(2,1)S(1)}, bf16[640]{0:T(1024)(128)(2,1)S(1)}...) all-reduce(bf16[640]{0:T(1024)(128)(2,1)S(1)} %dynamic-update-slice, ...), channel_id=1, replica_groups=mesh['narrow'=4,'wide'=8] {'wide'}, use_global_device_ids=true, to_apply=%add.3 | all-reduce | flops 5120 | bytes 20480
  82.4 9.5 %all-gather = bf16[8,1,640]{2,1,0:T(2,128)(2,1)S(1)} all-gather(bf16[1,1,640]{2,1,0:T(2,128)(2,1)S(1)} %reshape.230), channel_id=1, replica_groups=mesh['narrow'=4,'wide'=8] {'wide'}, dimensions={0}, use_global_device_ids=true | all-gather | bytes 11520 | tf_op jit(solution)/shard_map/all_gather | solution.py:116
  92.5 12.8 %all_gather.47 = bf16[640,640]{1,0:T(8,128)(2,1)} all-gather(bf16[80,640]{1,0:T(8,128)(2,1)S(1)} %copy-done.25), channel_id=1, replica_groups=mesh['narrow'=4,'wide'=8] {'wide'}, dimensions={0}, use_global_device_ids=true | all-gather | bytes 921600 | tf_op jit(solution)/shard_map/all_gather | solution.py:76
  106.2 4.7 maximum_select_fusion.2
  111.9 5.1 add_convert_fusion.1
  130.4 3.9 fusion.36
  135.7 30.6 %multiply_convert_fusion.1 = (bf16[512,5120]{1,0:T(8,128)(2,1)S(1)}, f32[512,5120]{1,0:T(8,128)}, f32[512,5120]{1,0:T(8,128)}) fusion(f32[5120]{0:T(1024)S(1)} %bitcast.121, bf16[640,5120]{1,0:T(8,128)(2,1)} %all-gather.7.cloned.1.call-done, f32[512,640]{1,0:T(8,128)S(1)} %get-tuple-element.124, f32[640]{0:T(1024)S(1)} %convert_element_type.218, ...), kind=kOutput, calls=%fused_computation.14 | convolution fusion | flops 3530096640 | bytes 34108416 | tf_op jit(solution)/shard_map/dot_general | solution.py:124
  166.3 44.4 %collective-permute-done.2 = bf16[2560,640]{1,0:T(8,128)(2,1)} collective-permute-done((bf16[2560,640]{1,0:T(8,128)(2,1)}, bf16[2560,640]{1,0:T(8,128)(2,1)}, u32[]{:S(2)}, u32[]{:S(2)}) %collective-permute-start.2) | collective-permute-done | bytes 3276832 | tf_op jit(solution)/shard_map/ppermute | solution.py:15
  210.7 9.1 %fusion.32 = bf16[512,640]{1,0:T(8,128)(2,1)S(1)} fusion(f32[512,640]{1,0:T(8,128)S(1)} %get-tuple-element.124, bf16[512,5120]{1,0:T(8,128)(2,1)S(1)} %get-tuple-element.115, bf16[2560,640]{1,0:T(8,128)(2,1)} %collective-permute-done.2, bf16[2560,640]{1,0:T(8,128)(2,1)} %maximum_select_fusion.2, pred[]{:T(512)S(6)} %eq.63, f32[640]{0:T(1024)S(1)} %convert_element_type.222), kind=kOutput, calls=%fused_computation.60 | convolution fusion | flops 3385917440 | bytes 13765121 | tf_op jit(solution)/shard_map/dot_general | solution.py:131
  221.0 14.8 %convert_reduce_fusion = (f32[5120]{0:T(1024)S(1)}, bf16[512,5120]{1,0:T(8,128)(2,1)}) fusion(f32[512,5120]{1,0:T(8,128)} %get-tuple-element.116, bf16[5120,640]{1,0:T(8,128)(2,1)} %all-gather.9.cloned.1.call-done, f32[512,640]{1,0:T(8,128)S(1)} %fusion.47, f32[512,5120]{1,0:T(8,128)} %get-tuple-element.125, f32[5120]{0:T(1024)S(1)} %bitcast.122), kind=kOutput, calls=%fused_computation.11 | convolution fusion | flops 3400330240 | bytes 34119680 | tf_op jit(solution)/shard_map/ld,fd->lf/dot_general | solution.py:161
  235.8 8.5 %multiply_reduce_fusion.1 = (f32[640]{0:T(1024)S(1)}, f32[512]{0:T(512)S(1)}, f32[640]{0:T(1024)S(1)}, f32[512,640]{1,0:T(8,128)S(1)}) fusion(f32[512,640]{1,0:T(8,128)S(1)} %copy-done.4, f32[512]{0:T(512)S(1)} %fusion.53, f32[512]{0:T(512)S(1)} %broadcast_multiply_fusion, f32[640]{0:T(1024)S(1)} %convert_element_type.217, ...), kind=kOutput, calls=%fused_computation.70 | convolution fusion | flops 3358063104 | bytes 14431744 | tf_op jit(solution)/shard_map/lf,df->ld/dot_general | solution.py:169
  252.0 13.9 %multiply_reduce_fusion = (f32[20,512]{1,0:T(8,128)S(1)}, f32[20,512,512]{1,2,0:T(8,128)}) fusion(f32[20,512,512]{1,2,0:T(8,128)} %copy-done.2, f32[20,512]{1,0:T(8,128)S(1)} %log_add_fusion, bf16[512,20,32]{0,2,1:T(8,128)(2,1)} %bitcast.110, bf16[512,3,20,32]{0,3,2,1:T(8,128)(2,1)S(1)} %bitcast.107), kind=kOutput, calls=%fused_computation.1 | convolution fusion | flops 351262720 | bytes 43343872 | tf_op jit(solution)/shard_map/while/body/eval_jaxpr/qhd,khd->hqk/dot_general | solution.py:207
  265.9 14.9 %multiply_convert_fusion = bf16[20,512,512]{1,2,0:T(8,128)(2,1)S(1)} fusion(f32[20,512,512]{1,2,0:T(8,128)} %get-tuple-element.130, f32[20,512,512]{1,2,0:T(8,128)} %copy-done.2, f32[20,512]{1,0:T(8,128)S(1)} %get-tuple-element.129, f32[20,512]{1,0:T(8,128)S(1)} %log_add_fusion), kind=kLoop, calls=%fused_computation | loop fusion | flops 20971520 | bytes 52510720 | tf_op jit(solution)/shard_map/while/body/eval_jaxpr/convert_element_type | solution.py:211
  285.6 9.1 %fusion.33 = bf16[20,32,512]{2,1,0:T(8,128)(2,1)S(1)} fusion(bf16[512,20,32]{0,2,1:T(8,128)(2,1)S(1)} %bitcast.111, f32[20,512,512]{1,2,0:T(8,128)} %copy-done.2, f32[20,512]{1,0:T(8,128)S(1)} %log_add_fusion), kind=kOutput, calls=%fused_computation.61 | convolution fusion | flops 346357760 | bytes 22323200 | tf_op jit(solution)/shard_map/while/body/eval_jaxpr/hqk,qhd->khd/dot_general | solution.py:201
  295.5 4.1 fusion.42
  301.0 12.3 %fusion.66 = f32[640,5120]{1,0:T(8,128)} fusion(bf16[512,5120]{1,0:T(8,128)(2,1)} %get-tuple-element.133, f32[512,640]{1,0:T(8,128)S(1)} %copy-done.5, f32[640]{0:T(1024)S(1)} %convert_element_type.218, f32[640]{0:T(1024)S(1)} %convert_element_type.217, f32[512]{0:T(512)S(1)} %fusion.53, f32[512]{0:T(512)S(1)} %broadcast_multiply_fusion), kind=kOutput, calls=%fused_computation.128 | convolution fusion | flops 3357081600 | bytes 19670016 | tf_op jit(solution)/shard_map/ld,lf->df/dot_general | solution.py:165
  313.3 12.1 %fusion.57 = f32[5120,640]{1,0:T(8,128)} fusion(bf16[512,5120]{1,0:T(8,128)(2,1)} %copy-done.11, f32[512,640]{1,0:T(8,128)S(1)} %fusion.47), kind=kOutput, calls=%fused_computation.122 | convolution fusion | flops 3355770880 | bytes 19660800 | tf_op jit(solution)/shard_map/lf,ld->fd/dot_general | solution.py:157
  327.4 27.5 %reduce-scatter.5.cloned.1.call-done = f32[80,1920]{1,0:T(8,128)} async-done(((f32[640,1920]{1,0:T(8,128)}), f32[80,1920]{1,0:T(8,128)}) %reduce-scatter.5.cloned.1.call-update) | async-done | bytes 614416 | tf_op jit(solution)/shard_map/reduce_scatter | solution.py:252
  356.7 96.4 %reduce-scatter.9.cloned.1.call-done = f32[80,5120]{1,0:T(8,128)} async-done(((f32[640,5120]{1,0:T(8,128)}), f32[80,5120]{1,0:T(8,128)}) %reduce-scatter.9.cloned.1.call-update) | async-done | bytes 1638416 | tf_op jit(solution)/shard_map/reduce_scatter | solution.py:175
  455.5 95.9 %reduce-scatter.11.cloned.1.call-done = f32[640,640]{1,0:T(8,128)} async-done(((f32[5120,640]{1,0:T(8,128)}), f32[640,640]{1,0:T(8,128)}) %reduce-scatter.11.cloned.1.call-update) | async-done | bytes 1638416 | tf_op jit(solution)/shard_map/reduce_scatter | solution.py:177
  556.7 4.0 fusion.68
  564.5 25.0 %all-reduce.19 = (bf16[640]{0:T(1024)(128)(2,1)S(1)}, bf16[640]{0:T(1024)(128)(2,1)S(1)}, bf16[640]{0:T(1024)(128)(2,1)S(1)}, bf16[640]{0:T(1024)(128)(2,1)S(1)}...) all-reduce(f32[640]{0:T(1024)S(1)} %get-tuple-element.70, ...), channel_id=2, replica_groups=mesh['narrow'=4,'wide'=8] {'wide'}, use_global_device_ids=true, to_apply=%region_14.15.clone | all-reduce | flops 10256 | bytes 61536
  592.6 12.5 %all-reduce.21 = (bf16[80]{0:T(256)(128)(2,1)S(1)}, bf16[80]{0:T(256)(128)(2,1)S(1)}, bf16[80]{0:T(256)(128)(2,1)S(1)}, bf16[80]{0:T(256)(128)(2,1)S(1)}, bf16[8...) all-reduce(bf16[80]{0:T(256)(128)(2,1)S(1)} %dynamic-slice.47, ...), channel_id=1, replica_groups=mesh['narrow'=4,'wide'=8] {'narrow'}, use_global_device_ids=true, to_apply=%region_15.16 | all-reduce | flops 1282 | bytes 5128 | tf_op jit(solution)/shard_map/psum | solution.py:259
  611.1 29.3 %all-reduce.25.cloned.1.call-done = (bf16[80,1920]{1,0:T(8,128)(2,1)}, bf16[80,640]{1,0:T(8,128)(2,1)}, bf16[80,5120]{1,0:T(8,128)(2,1)}, bf16[640,640]{1,0:T(8,128)(2,1)}) async-done(((bf16[80,1920]{1,0:T(8,128)(2,1)}, bf16[80,640]{1,0:T(8,128)(2,1)}, bf16[80,5120]{1,0:T(8,128)(2,1)}, bf16[640,640]{1,0:T(8,128)(2,1)}), (bf16[80,1920]{1,0:T(8,128)(2,1)}, bf16[80,640]{1,0:T(8,128)(2,1)}, ...) | async-done | bytes 2048016 | tf_op jit(solution)/shard_map/psum | solution.py:261
  (216 shorter events, 73.4 us)
Async XLA Ops:
  7.2 212.6 %copy-start = (bf16[640,25]{0,1:T(8,128)(2,1)S(1)}, bf16[640,25]{0,1:T(8,128)(2,1)}, u32[]{:S(2)}) copy-start(bf16[640,25]{0,1:T(8,128)(2,1)} %param.22) | copy-start | bytes 96004
  7.3 84.6 %copy-start.8 = (bf16[1,512,640]{2,1,0:T(8,128)(2,1)S(1)}, bf16[1,512,640]{2,1,0:T(8,128)(2,1)}, u32[]{:S(2)}) copy-start(bf16[1,512,640]{2,1,0:T(8,128)(2,1)} %param.18) | copy-start | bytes 1966084
  7.3 85.1 %copy-start.25 = (bf16[80,640]{1,0:T(8,128)(2,1)S(1)}, bf16[80,640]{1,0:T(8,128)(2,1)}, u32[]{:S(2)}) copy-start(bf16[80,640]{1,0:T(8,128)(2,1)} %param.28) | copy-start | bytes 307204
  7.3 97.9 %copy-start.34 = (s32[1,512]{1,0:T(1,128)S(1)}, s32[1,512]{1,0:T(1,128)}, u32[]{:S(2)}) copy-start(s32[1,512]{1,0:T(1,128)} %param.19) | copy-start | bytes 6148
  7.4 104.5 %all-gather.5.cloned.1.call-start = ((), (), s32[]{:S(2)}) async-start(), calls=%async_computation.4 | async-start | bytes 2764800 | tf_op jit(solution)/shard_map/all_gather | solution.py:73
  8.1 127.5 %all-gather.7.cloned.1.call-start = ((), (), s32[]{:S(2)}) async-start(), calls=%async_computation.5 | async-start | bytes 7372800 | tf_op jit(solution)/shard_map/all_gather | solution.py:115
  8.8 212.2 %all-gather.9.cloned.1.call-start = ((), (), s32[]{:S(2)}) async-start(), calls=%async_computation.6 | async-start | bytes 7372800 | tf_op jit(solution)/shard_map/all_gather | solution.py:154
  8.9 2.7 collective-permute-start
  13.6 92.6 %collective-permute-start.1 = (bf16[1280,640]{1,0:T(8,128)(2,1)S(1)}, bf16[1280,640]{1,0:T(8,128)(2,1)}, u32[]{:S(2)}, u32[]{:S(2)}) collective-permute-start(bf16[1280,640]{1,0:T(8,128)(2,1)S(1)} %maximum_select_fusion.3), channel_id=1, source_target_pairs={{0,2},{1,3},{2,0},{3,1},{4,6},{5,7},{6,4},{7,5},{8,10},{9,11},{10,... | collective-permute-start | bytes 4915208 | tf_op jit(solution)/shard_map/ppermute | solution.py:15
  16.5 309.2 %reduce-scatter.7.cloned.1.call-start = ((), (), s32[]{:S(2)}) async-start(), calls=%async_computation.8 | async-start | bytes 1843200 | tf_op jit(solution)/shard_map/reduce_scatter | solution.py:255
  82.3 29.6 %copy-start.26 = (f32[640]{0:T(1024)}, f32[640]{0:T(1024)S(1)}, u32[]{:S(2)}) copy-start(f32[640]{0:T(1024)S(1)} %convert_element_type.208) | copy-start | bytes 7684
  82.3 29.6 %copy-start.38 = (f32[640]{0:T(1024)}, f32[640]{0:T(1024)S(1)}, u32[]{:S(2)}) copy-start(f32[640]{0:T(1024)S(1)} %convert_element_type.209) | copy-start | bytes 7684
  92.4 24.6 %copy-start.30 = (f32[512]{0:T(512)}, f32[512]{0:T(512)S(1)}, u32[]{:S(2)}) copy-start(f32[512]{0:T(512)S(1)} %fusion.40) | copy-start | bytes 6148
  110.8 99.8 %collective-permute-start.2 = (bf16[2560,640]{1,0:T(8,128)(2,1)}, bf16[2560,640]{1,0:T(8,128)(2,1)}, u32[]{:S(2)}, u32[]{:S(2)}) collective-permute-start(bf16[2560,640]{1,0:T(8,128)(2,1)} %maximum_select_fusion.2), channel_id=1, source_target_pairs={{0,4},{1,5},{2,6},{3,7},{4,0},{5,1},{6,2},{7,3},{8,12},{9,13},{10,... | collective-permute-start | bytes 9830408 | tf_op jit(solution)/shard_map/ppermute | solution.py:15
  135.3 75.4 %copy-start.3 = (f32[512,640]{1,0:T(8,128)}, f32[512,640]{1,0:T(8,128)S(1)}, u32[]{:S(2)}) copy-start(f32[512,640]{1,0:T(8,128)S(1)} %get-tuple-element.124) | copy-start | bytes 3932164
  166.3 53.5 %copy-start.11 = (bf16[512,5120]{1,0:T(8,128)(2,1)}, bf16[512,5120]{1,0:T(8,128)(2,1)S(1)}, u32[]{:S(2)}) copy-start(bf16[512,5120]{1,0:T(8,128)(2,1)S(1)} %get-tuple-element.115) | copy-start | bytes 15728644
  252.0 102.8 %reduce-scatter.5.cloned.1.call-start = ((), (), s32[]{:S(2)}) async-start(), calls=%async_computation.7 | async-start | bytes 5529600 | tf_op jit(solution)/shard_map/reduce_scatter | solution.py:252
  299.7 153.4 %reduce-scatter.9.cloned.1.call-start = ((), (), s32[]{:S(2)}) async-start(), calls=%async_computation.9 | async-start | bytes 14745600 | tf_op jit(solution)/shard_map/reduce_scatter | solution.py:175
  313.2 238.2 %reduce-scatter.11.cloned.1.call-start = ((), (), s32[]{:S(2)}) async-start(), calls=%async_computation.10 | async-start | bytes 14745600 | tf_op jit(solution)/shard_map/reduce_scatter | solution.py:177
  325.4 314.9 %all-reduce.25.cloned.1.call-start = ((), (), s32[]{:S(2)}) async-start(), calls=%async_computation.11 | async-start | bytes 4096000 | tf_op jit(solution)/shard_map/psum | solution.py:261
  327.4 227.8 %copy-start.37 = (s32[1,512]{1,0:T(1,128)S(1)}, s32[1,512]{1,0:T(1,128)}, u32[]{:S(2)}) copy-start(s32[1,512]{1,0:T(1,128)} %param.21) | copy-start | bytes 6148
  327.4 229.0 %copy-start.14 = (bf16[20,32,512]{2,1,0:T(8,128)(2,1)S(1)}, bf16[20,32,512]{2,1,0:T(8,128)(2,1)}, u32[]{:S(2)}) copy-start(bf16[20,32,512]{2,1,0:T(8,128)(2,1)} %copy-done.13) | copy-start | bytes 1966084
  327.4 229.0 %copy-start.16 = (bf16[20,32,512]{2,1,0:T(8,128)(2,1)S(1)}, bf16[20,32,512]{2,1,0:T(8,128)(2,1)}, u32[]{:S(2)}) copy-start(bf16[20,32,512]{2,1,0:T(8,128)(2,1)} %copy-done.15) | copy-start | bytes 1966084
  561.5 86.1 %copy-start.1 = (bf16[640,25]{0,1:T(8,128)(2,1)S(1)}, bf16[640,25]{0,1:T(8,128)(2,1)}, u32[]{:S(2)}) copy-start(bf16[640,25]{0,1:T(8,128)(2,1)} %param.22) | copy-start | bytes 96004
  (37 other events, 288.7 us)
Sparse Core Ops, SparseCore 0:
  10.0 41.9 all-gather.4
  53.9 47.8 all-gather.6
  103.7 73.1 all-gather.8
  252.1 38.8 reduce-scatter.6
  299.8 55.0 reduce-scatter.4
  358.3 94.7 reduce-scatter.8
  456.6 94.7 reduce-scatter.10
  555.2 85.1 all-reduce.24
